TPU v7x, 32 devices: a whole 2x2x4 slice. The times are simulated.
32 devices in a mesh: ia: 4 (over x, core), ja: 2 (over y), ka: 4 (over z).
Axes of the slice: x: 2, y: 2, z: 4, core: 2. Of those that a mesh axis runs over, the one named last changes fastest.
Arguments:
- tensor: float32 [128, 256, 512], P('ia', 'ja', 'ka'), may hold values from -200 to 200
- factor_b: float32 [256, 4, 96], P(('ja', 'ka')), may hold values from -4 to 4
- factor_c: float32 [512, 4, 96], P(('ka', 'ja')), may hold values from -4 to 4
Outputs:
- factor_a: float32 [128, 4, 96], P(('ia', 'ja', 'ka'))
- weights: float32 [4, 96], replicated
All inputs are finite; a program needn't handle non-finite values.
Results may differ from a plain program's by a relative error of at most 0.0003.
Values sent between devices are 32-bit elements; how exact they have to be, the bound alone decides.
A program may use at most 64 MiB of HBM per device.

v0:
```python
import jax
import jax.numpy as jnp
from jax import lax
from jax.sharding import PartitionSpec as P

highest = lax.Precision.HIGHEST


def gram_of(rows):
    return jnp.einsum(
        "jsr,jsq->srq", rows, rows, precision=highest, preferred_element_type=jnp.float32
    )


def solve_normal(rows, gram_b, gram_c):
    columns = []
    for member in range(rows.shape[1]):
        normal_mat = gram_b[member] * gram_c[member]
        factor_l = jnp.linalg.cholesky(normal_mat)
        right_side = rows[:, member, :].T
        lower_sol = lax.linalg.triangular_solve(factor_l, right_side, left_side=True, lower=True)
        upper_sol = lax.linalg.triangular_solve(
            factor_l, lower_sol, left_side=True, lower=True, transpose_a=True
        )
        columns.append(upper_sol.T)
    return jnp.stack(columns, axis=1)


def shards(tensor, factor_b, factor_c):
    rows_i, rows_j, rows_k = tensor.shape
    starts, col_count = (factor_b.shape[1], factor_b.shape[2])
    width = starts * col_count
    c_block = lax.all_gather(factor_c, "ja", axis=0, tiled=True)
    partial_value = jnp.dot(
        tensor.reshape(rows_i * rows_j, rows_k),
        c_block.reshape(rows_k, width),
        precision=highest,
        preferred_element_type=jnp.float32,
    ).reshape(rows_i, rows_j, width)
    piece = lax.all_gather(factor_b, "ka", axis=0, tiled=True)
    gram_sum = jnp.zeros((starts, col_count, col_count), jnp.float32)
    count = piece.shape[0]
    flat_rows = piece.reshape(count, width)
    mttkrp = jnp.einsum(
        "ijr,jr->ir",
        partial_value,
        flat_rows,
        precision=highest,
        preferred_element_type=jnp.float32,
    )
    mttkrp, gram_rows = (mttkrp, gram_sum)
    gram_b, gram_c = lax.psum((gram_of(factor_b), gram_of(factor_c)), ("ja", "ka"))
    owned = lax.psum_scatter(mttkrp, ("ja", "ka"), scatter_dimension=0, tiled=True)
    owned = owned.reshape(owned.shape[0], starts, col_count)
    factor_raw = solve_normal(owned, gram_b, gram_c)
    squares = jnp.sum(factor_raw * factor_raw, axis=0)
    total = lax.psum(squares, ("ia", "ja", "ka"))
    row_total = rows_i * lax.axis_size("ia")
    weights = jnp.sqrt(total / row_total + 1e-06)
    return (factor_raw / weights[None], weights)


def solution(mesh):
    in_specs = (P("ia", "ja", "ka"), P(("ja", "ka"), None, None), P(("ka", "ja"), None, None))
    out_specs = (P(("ia", "ja", "ka"), None, None), P())
    return jax.shard_map(shards, mesh=mesh, in_specs=in_specs, out_specs=out_specs, check_vma=False)
```

profile of v0, /device:TPU:0, one launch (start us, length us, event | category | flops | bytes accessed | tf_op | source)
XLA Modules:
  0.0 222.9 jit_solution(2822683292989447386)
XLA Ops:
  7.2 2.3 %fusion = f32[4,96,96]{1,2,0:T(8,128)} fusion(f32[64,4,96]{2,1,0:T(4,128)} %param.10), kind=kOutput, calls=%fused_computation.4 | convolution fusion | flops 28311552 | bytes 245760 | tf_op jit(solution)/shard_map/jsr,jsq->srq/dot_general | solution.py:10
  9.5 2.1 fusion.2
  11.6 7.4 %all_gather.6 = f32[128,4,96]{2,1,0:T(4,128)S(1)} all-gather(f32[64,4,96]{2,1,0:T(4,128)} %param.10), channel_id=1, replica_groups=mesh['ia'=4,'ja'=2,'ka'=4] {'ja'}, dimensions={0}, use_global_device_ids=true | all-gather | bytes 294912 | tf_op jit(solution)/shard_map/all_gather | solution.py:33
  19.1 15.1 %all_gather.7 = f32[128,4,96]{2,1,0:T(4,128)S(1)} all-gather(f32[32,4,96]{2,1,0:T(4,128)} %param.9), channel_id=1, replica_groups=mesh['ia'=4,'ja'=2,'ka'=4] {'ka'}, dimensions={0}, use_global_device_ids=true | all-gather | bytes 245760 | tf_op jit(solution)/shard_map/all_gather | solution.py:40
  34.3 7.1 %fusion.28 = f32[32,128,384]{2,1,0:T(8,128)} fusion(f32[32,128,128]{2,1,0:T(8,128)S(1)} %copy-done, f32[128,384,1]{0,1,2:T(8,128)S(1)} %bitcast.130), kind=kOutput, calls=%fused_computation.63 | convolution fusion | flops 2415919104 | bytes 8585216 | tf_op jit(solution)/shard_map/dot_general | solution.py:34
  41.3 6.7 %copy.46 = f32[32,128,384]{1,0,2:T(8,128)} copy(f32[32,128,384]{2,1,0:T(8,128)} %fusion.28) | data formatting | bytes 12582912 | tf_op jit(solution)/shard_map/dot_general | solution.py:34
  48.2 11.9 %fusion.29 = f32[384,1,32]{2,1,0:T(1,128)S(1)} fusion(f32[32,128,384]{1,0,2:T(8,128)} %copy.46, f32[128,384,1]{0,2,1:T(1,128)S(1)} %bitcast.124), kind=kOutput, calls=%fused_computation.64 | convolution fusion | flops 18874368 | bytes 6537216 | tf_op jit(solution)/shard_map/ijr,jr->ir/dot_general | solution.py:44
  61.3 41.9 %all-reduce = f32[32,384]{0,1:T(8,128)S(1)} all-reduce(f32[32,384]{0,1:T(8,128)S(1)} %bitcast.125), channel_id=2, replica_groups=mesh['ia'=4,'ja'=2,'ka'=4] {'ja','ka'}, use_global_device_ids=true, to_apply=%region_4.0.clone | all-reduce | flops 12288 | bytes 98304
  103.4 1.0 fusion.24
  104.7 1.0 fusion.15
  105.7 8.8 %cholesky.107 = f32[96,96]{1,0:T(8,128)S(1)} custom-call(f32[96,96]{1,0:T(8,128)S(1)} %get-tuple-element.14), custom_call_target="Cholesky" | custom-call | tf_op jit(solution)/shard_map/jit(cholesky)/cholesky | solution.py:19
  114.5 0.6 compare_reduce_fusion
  115.2 0.7 fusion.7
  115.9 7.4 %custom-call.21 = f32[1,96,96]{1,2,0:T(8,128)S(1)} custom-call(f32[1,96,96]{2,1,0:T(8,128)S(1)} %fusion.7), custom_call_target="InvertDiagBlocksLowerTriangular" | custom-call | tf_op jit(solution)/shard_map/triangular_solve/custom-call.2 | solution.py:22
  123.6 8.8 %cholesky.96 = f32[96,96]{1,0:T(8,128)S(1)} custom-call(f32[96,96]{1,0:T(8,128)S(1)} %get-tuple-element.15), custom_call_target="Cholesky" | custom-call | tf_op jit(solution)/shard_map/jit(cholesky)/cholesky | solution.py:19
  133.1 0.7 fusion.6
  133.8 7.4 %custom-call.19 = f32[1,96,96]{1,2,0:T(8,128)S(1)} custom-call(f32[1,96,96]{2,1,0:T(8,128)S(1)} %fusion.6), custom_call_target="InvertDiagBlocksLowerTriangular" | custom-call | tf_op jit(solution)/shard_map/triangular_solve/custom-call.2 | solution.py:22
  141.5 8.8 %cholesky.85 = f32[96,96]{1,0:T(8,128)S(1)} custom-call(f32[96,96]{1,0:T(8,128)S(1)} %get-tuple-element.16), custom_call_target="Cholesky" | custom-call | tf_op jit(solution)/shard_map/jit(cholesky)/cholesky | solution.py:19
  151.0 0.7 fusion.5
  151.7 7.4 %custom-call.17 = f32[1,96,96]{1,2,0:T(8,128)S(1)} custom-call(f32[1,96,96]{2,1,0:T(8,128)S(1)} %fusion.5), custom_call_target="InvertDiagBlocksLowerTriangular" | custom-call | tf_op jit(solution)/shard_map/triangular_solve/custom-call.2 | solution.py:22
  159.5 9.0 %cholesky.74 = f32[96,96]{1,0:T(8,128)S(1)} custom-call(f32[96,96]{1,0:T(8,128)S(1)} %get-tuple-element.13), custom_call_target="Cholesky" | custom-call | tf_op jit(solution)/shard_map/jit(cholesky)/cholesky | solution.py:19
  169.2 0.7 fusion.4
  169.8 7.4 %custom-call.15 = f32[1,96,96]{1,2,0:T(8,128)S(1)} custom-call(f32[1,96,96]{2,1,0:T(8,128)S(1)} %fusion.4), custom_call_target="InvertDiagBlocksLowerTriangular" | custom-call | tf_op jit(solution)/shard_map/triangular_solve/custom-call.2 | solution.py:22
  177.6 37.8 %psum.23 = f32[4,96]{1,0:T(4,128)S(1)} all-reduce(f32[4,96]{1,0:T(4,128)S(1)} %multiply_reduce_fusion), channel_id=1, replica_groups=mesh['ia'=4,'ja'=2,'ka'=4] {'ia','ja','ka'}, use_global_device_ids=true, to_apply=%region_6.10 | all-reduce | flops 384 | bytes 3072 | tf_op jit(solution)/shard_map/psum | solution.py:57
  (36 shorter events, 5.7 us)
Async XLA Ops:
  7.2 27.1 %copy-start = (f32[32,128,128]{2,1,0:T(8,128)S(1)}, f32[32,128,128]{2,1,0:T(8,128)}, u32[]{:S(2)}) copy-start(f32[32,128,128]{2,1,0:T(8,128)} %param.8) | copy-start | bytes 6291460
  7.2 96.2 %all-reduce.4.cloned.1.call-start = ((), (), s32[]{:S(2)}) async-start(), calls=%async_computation | async-start | bytes 786432 | tf_op jit(solution)/shard_map/psum | solution.py:52
  48.0 12.0 %copy-start.2 = (u32[32]{0:T(128)S(1)}, u32[32]{0:T(128)}, u32[]{:S(2)}) copy-start(u32[32]{0:T(128)} %constant.41) | copy-start | bytes 388
  215.4 0.6 copy-start.1
Sparse Core Ops, SparseCore 0:
  11.8 75.5 all-reduce.3
where the time goes:
time: 223 us
  blocking collectives  102 us (46%)
  other arithmetic  72.3 us (32%)
  matrix products  24.9 us (11%)
  between operations  14.9 us (7%)
  local copies, waits for them, and re-layouts  8.59 us (4%)
    unnamed x1, blocking collectives  41.9 us
    another operation x12, other arithmetic, solve_normal(): factor_l = jnp.linalg.cholesky(normal_mat)  38.1 us
    psum x1, blocking collectives, shards(): total = lax.psum(squares, ('ia', 'ja', 'ka'))  37.8 us
    another operation x8, other arithmetic, solve_normal(): lax.linalg.triangular_solve(factor_l, lower_sol, left_side=True, lower=Tr...  32 us
    all_gather x1, blocking collectives, shards(): piece = lax.all_gather(factor_b, 'ka', axis=0, tiled=True)  15.1 us
    dot_general x1, matrix products, shards(): jnp.einsum('ijr,jr->ir', partial_value, flat_rows, precision=highest, pre...  11.9 us
    all_gather x1, blocking collectives, shards(): c_block = lax.all_gather(factor_c, 'ja', axis=0, tiled=True)  7.42 us
    dot_general x1, matrix products, shards(): jnp.dot(tensor.reshape(rows_i * rows_j, rows_k), c_block.reshape(rows_k,...  7.07 us
  transfers between devices with their start and end apart: 1, of which 0 were waited for; matrix products, arithmetic and copies ran while one was open for 12% of the time, Pallas kernels for 0%

commit v1 on v0

v1 whole, which is shorter than its diff:
```python
import functools

import jax
import jax.numpy as jnp
from jax import lax
from jax.experimental import pallas as pl
from jax.experimental.pallas import tpu as pltpu
from jax.sharding import PartitionSpec as P

MESH = pl.DeviceIdType.MESH
LANES = 128
SUBS = 8
HIGHEST = lax.Precision.HIGHEST


def solver_places(sizes, starts):
    na, nj, nk = sizes
    places = []
    for s in range(starts):
        ia = (s % 2) * (na // 2)
        ja = ((s // 2) * (nj // 2)) % nj
        ka = min(nk - 1, max(0, nk // 2 - 1 + (s // 2) % 2))
        places.append((ia, ja, ka))
    assert len(set(places)) == starts
    return places


def negative_inverse(tiles, cols):
    lane = lax.broadcasted_iota(jnp.int32, (SUBS, LANES), 1)
    sub = lax.broadcasted_iota(jnp.int32, (SUBS, LANES), 0)
    for k in range(0, cols, 2):
        v, p = k // SUBS, k % SUBS
        at0, at1 = lane == k, lane == k + 1
        both = at0 | at1
        row0 = jnp.broadcast_to(tiles[v][p : p + 1, :], (SUBS, LANES))
        row1 = jnp.broadcast_to(tiles[v][p + 1 : p + 2, :], (SUBS, LANES))
        col0 = [jnp.broadcast_to(t[:, k : k + 1], (SUBS, LANES)) for t in tiles]
        col1 = [jnp.broadcast_to(t[:, k + 1 : k + 2], (SUBS, LANES)) for t in tiles]
        a = jnp.broadcast_to(row0[:, k : k + 1], (SUBS, LANES))
        b = jnp.broadcast_to(row0[:, k + 1 : k + 2], (SUBS, LANES))
        d = jnp.broadcast_to(row1[:, k + 1 : k + 2], (SUBS, LANES))
        inv_a = 1.0 / a
        t = b * inv_a
        inv_s = 1.0 / (d - b * t)
        row0 = jnp.where(at0, -1.0, jnp.where(at1, 0.0, row0))
        row1 = jnp.where(at1, -1.0, jnp.where(at0, 0.0, row1))
        new1 = (row1 - t * row0) * inv_s
        new0 = row0 * inv_a - t * new1
        out = []
        for i, tile in enumerate(tiles):
            new = jnp.where(both, 0.0, tile) - col0[i] * new0 - col1[i] * new1
            if i == v:
                new = jnp.where(sub == p, new0, jnp.where(sub == p + 1, new1, new))
            out.append(new)
        tiles = out
    return tiles


def split(x):
    hi = x.astype(jnp.bfloat16)
    return hi, (x - hi.astype(jnp.float32)).astype(jnp.bfloat16)


def kernel(sizes, places, total_rows, t_ref, b_ref, c_ref, out_ref, w_ref,
           bg, cg, gb, gc, mp, mr, ob, orx,
           bs, br, cs, cr, gs, gbr, gcr, ms, mrs, os, ors):
    na, nj, nk = sizes
    group = nj * nk
    n = na * group
    starts, cols = b_ref.shape[1], b_ref.shape[2]
    rows_i = t_ref.shape[0]
    own_rows = out_ref.shape[0]
    ia, ja, ka = (lax.axis_index("ia"), lax.axis_index("ja"), lax.axis_index("ka"))
    g = ja * nk + ka
    me = ia * group + g
    ids = [(pa * nj + pj) * nk + pk for pa, pj, pk in places]

    def coords(d):
        return (d // group, (d // nk) % nj, d % nk)

    barrier = pltpu.get_barrier_semaphore()

    def greet(target):
        pl.semaphore_signal(barrier, inc=1, device_id=target, device_id_type=MESH)

    for o in range(1, nk):
        greet((ia, ja, lax.rem(ka + o, nk)))
    for o in range(1, nj):
        greet((ia, lax.rem(ja + o, nj), ka))
    for s, place in enumerate(places):
        @pl.when(me != ids[s])
        def _():
            greet(place)

        @pl.when(me == ids[s])
        def _():
            @pl.loop(1, n)
            def _(o):
                greet(coords(lax.rem(me + o, n)))

    for s in range(starts):
        bg[ka, s] = jnp.zeros(bg.shape[2:], jnp.float32)
        cg[ja, s] = jnp.zeros(cg.shape[2:], jnp.float32)
        bg[ka, s, :, 0:cols] = b_ref[:, s, :]
        cg[ja, s, :, 0:cols] = c_ref[:, s, :]

    is_solver = functools.reduce(jnp.logical_or, [me == d for d in ids])
    near = (nk - 1) + (nj - 1)

    @pl.when(is_solver)
    def _():
        pl.semaphore_wait(barrier, near + starts - 1 + n - 1)

    @pl.when(jnp.logical_not(is_solver))
    def _():
        pl.semaphore_wait(barrier, near + starts)

    def push(src, dst, send, recv, place, target_id, act):
        @pl.when(me == target_id)
        def _():
            if act == "start":
                pltpu.make_async_copy(src, dst, recv).start()

        @pl.when(me != target_id)
        def _():
            copy = pltpu.make_async_remote_copy(
                src_ref=src, dst_ref=dst, send_sem=send, recv_sem=recv,
                device_id=place, device_id_type=MESH)
            if act == "start":
                copy.start()
            else:
                copy.wait_send()

    def gram_rows(act):
        for s, place in enumerate(places):
            @pl.when(ia == place[0])
            def _():
                push(bg.at[ka, s], gb.at[g], gs.at[s], gbr, place, ids[s], act)

            @pl.when(ia == place[0] + 1)
            def _():
                push(cg.at[ja, s], gc.at[g], gs.at[s], gcr, place, ids[s], act)

    gram_rows("start")
    c_copies = []
    for o in range(1, nj):
        c_copies.append(pltpu.make_async_remote_copy(
            src_ref=cg.at[ja], dst_ref=cg.at[ja], send_sem=cs.at[o - 1], recv_sem=cr.at[o - 1],
            device_id=(ia, lax.rem(ja + o, nj), ka), device_id_type=MESH))
    b_copies = []
    for o in range(1, nk):
        b_copies.append(pltpu.make_async_remote_copy(
            src_ref=bg.at[ka], dst_ref=bg.at[ka], send_sem=bs.at[o - 1], recv_sem=br.at[o - 1],
            device_id=(ia, ja, lax.rem(ka + o, nk)), device_id_type=MESH))
    for copy in c_copies + b_copies:
        copy.start()
    for o in range(1, nj):
        src = cg.at[lax.rem(ja - o + nj, nj)]
        pltpu.make_async_copy(src, src, cr.at[o - 1]).wait()
    for o in range(1, nk):
        src = bg.at[lax.rem(ka - o + nk, nk)]
        pltpu.make_async_copy(src, src, br.at[o - 1]).wait()

    c_all = [jnp.concatenate([cg[q, s] for q in range(nj)], axis=0) for s in range(starts)]
    c_hi, c_lo = split(jnp.concatenate(c_all, axis=1))
    c_twice = jnp.concatenate([c_hi, c_hi], axis=0)
    b_all = jnp.concatenate(
        [jnp.concatenate([bg[q, s] for q in range(nk)], axis=0) for s in range(starts)], axis=1)
    rows_j, rows_k = t_ref.shape[1], t_ref.shape[2]
    step = SUBS

    @pl.loop(0, rows_i // step)
    def _(block):
        at = pl.multiple_of(block * step, step)
        t_hi, t_lo = split(t_ref[pl.ds(at, step)].reshape(step * rows_j, rows_k))
        part = jnp.dot(jnp.concatenate([t_hi, t_lo], axis=1), c_twice,
                       preferred_element_type=jnp.float32)
        part = part + jnp.dot(t_hi, c_lo, preferred_element_type=jnp.float32)
        summed = jnp.sum(part.reshape(step, rows_j, starts * LANES) * b_all[None], axis=1)
        for s in range(starts):
            mp[s, pl.ds(at, step), :] = summed[:, s * LANES : (s + 1) * LANES]

    def mttkrp_rows(act):
        for s, place in enumerate(places):
            push(mp.at[s], mr.at[me], ms.at[s], mrs, place, ids[s], act)

    mttkrp_rows("start")

    @pl.when(is_solver)
    def _():
        pltpu.make_async_copy(gb, gb, gbr).wait()
        pltpu.make_async_copy(gc, gc, gcr).wait()
        over_rows = (((0,), (0,)), ((), ()))
        rows_b = gb[...].reshape(gb.shape[0] * gb.shape[1], LANES)
        rows_c = gc[...].reshape(gc.shape[0] * gc.shape[1], LANES)
        gram_b = lax.dot_general(rows_b, rows_b, over_rows, precision=HIGHEST,
                                 preferred_element_type=jnp.float32)
        gram_c = lax.dot_general(rows_c, rows_c, over_rows, precision=HIGHEST,
                                 preferred_element_type=jnp.float32)
        normal = gram_b * gram_c
        tiles = [normal[i : i + SUBS, :] for i in range(0, cols, SUBS)]
        tiles = negative_inverse(tiles, cols)
        minus = jnp.concatenate(
            tiles + [jnp.zeros((LANES - cols, LANES), jnp.float32)], axis=0)

        pltpu.make_async_copy(mr, mr, mrs).wait()
        blocks = []
        for q in range(na):
            blocks.append(lax.fori_loop(
                1, group, lambda h, acc, q=q: acc + mr[q * group + h], mr[q * group]))
        mttkrp = jnp.concatenate(blocks, axis=0)
        raw = -jnp.dot(mttkrp, minus, precision=HIGHEST, preferred_element_type=jnp.float32)
        weight = jnp.sqrt(jnp.sum(raw * raw, axis=0, keepdims=True) / total_rows + 1e-06)
        final = raw / weight
        for d in range(n):
            ob[d, 0:own_rows, :] = final[d * own_rows : (d + 1) * own_rows, :]
            ob[d, own_rows : own_rows + 1, :] = weight

        for s in range(starts):
            @pl.when(me == ids[s])
            def _():
                pltpu.make_async_copy(ob.at[me], orx.at[s], ors.at[s]).start()

                @pl.loop(1, n)
                def _(o):
                    d = lax.rem(me + o, n)
                    pltpu.make_async_remote_copy(
                        src_ref=ob.at[d], dst_ref=orx.at[s], send_sem=os, recv_sem=ors.at[s],
                        device_id=coords(d), device_id_type=MESH).start()

    for s in range(starts):
        pltpu.make_async_copy(orx.at[s], orx.at[s], ors.at[s]).wait()
        out_ref[:, s, :] = orx[s, 0:own_rows, 0:cols]
        w_ref[s : s + 1, :] = orx[s, own_rows : own_rows + 1, 0:cols]

    gram_rows("wait")
    mttkrp_rows("wait")
    for copy in c_copies + b_copies:
        copy.wait_send()

    @pl.when(is_solver)
    def _():
        rest = ob.at[pl.ds(0, n - 1)]
        pltpu.make_async_copy(rest, rest, os).wait()


def shards(sizes, tensor, factor_b, factor_c):
    na, nj, nk = sizes
    group = nj * nk
    n = na * group
    rows_i = tensor.shape[0]
    rows_b, starts, cols = factor_b.shape
    rows_c = factor_c.shape[0]
    own_rows = rows_i // group
    deep = -(-(own_rows + 1) // SUBS) * SUBS
    places = solver_places(sizes, starts)
    dma = pltpu.SemaphoreType.DMA
    f32 = jnp.float32
    vmem = pl.BlockSpec(memory_space=pltpu.VMEM)
    return pl.pallas_call(
        functools.partial(kernel, sizes, places, rows_i * na),
        out_shape=(
            jax.ShapeDtypeStruct((own_rows, starts, cols), f32),
            jax.ShapeDtypeStruct((starts, cols), f32),
        ),
        in_specs=[vmem] * 3,
        out_specs=(vmem, vmem),
        scratch_shapes=[
            pltpu.VMEM((nk, starts, rows_b, LANES), f32),
            pltpu.VMEM((nj, starts, rows_c, LANES), f32),
            pltpu.VMEM((group, rows_b, LANES), f32),
            pltpu.VMEM((group, rows_c, LANES), f32),
            pltpu.VMEM((starts, rows_i, LANES), f32),
            pltpu.VMEM((n, rows_i, LANES), f32),
            pltpu.VMEM((n, deep, LANES), f32),
            pltpu.VMEM((starts, deep, LANES), f32),
            dma((max(nk - 1, 1),)), dma((max(nk - 1, 1),)),
            dma((max(nj - 1, 1),)), dma((max(nj - 1, 1),)),
            dma((starts,)), dma, dma,
            dma((starts,)), dma,
            dma, dma((starts,)),
        ],
        compiler_params=pltpu.CompilerParams(collective_id=0, has_side_effects=True),
        name="factor_update",
    )(tensor, factor_b, factor_c)


def solution(mesh):
    sizes = (mesh.shape["ia"], mesh.shape["ja"], mesh.shape["ka"])
    in_specs = (P("ia", "ja", "ka"), P(("ja", "ka"), None, None), P(("ka", "ja"), None, None))
    out_specs = (P(("ia", "ja", "ka"), None, None), P())
    return jax.shard_map(functools.partial(shards, sizes), mesh=mesh, in_specs=in_specs,
                         out_specs=out_specs, check_vma=False)
```

time: 223 us -> 35.4 us (0.16)
  blocking collectives: 102 us -> 0 us
  other arithmetic: 72.3 us -> 0 us
  Pallas kernels: 0 us -> 32 us
  matrix products: 24.9 us -> 0 us
  between operations: 14.9 us -> 0.64 us
  local copies, waits for them, and re-layouts: 8.59 us -> 2.53 us
    another operation x20 -> x0, other arithmetic: 70.2 us -> none  [the longest x12 38.1 us: solve_normal(): factor_l = jnp.linalg.cholesky(normal_mat)]
    unnamed x1 -> x0, blocking collectives: 41.9 us -> none
    psum x1 -> x0, blocking collectives: 37.8 us -> none  [shards(): total = lax.psum(squares, ('ia', 'ja', 'ka'))]
    pallas_call x0 -> x1, Pallas kernels: none -> 32 us  [shards(): pl.pallas_call(functools.partial(kernel, sizes, places, rows_i * na), out...]
    dot_general x4 -> x0, matrix products: 23.3 us -> none  [the longest x1 11.9 us: shards(): jnp.einsum('ijr,jr->ir', partial_value, flat_rows, precision=highest, pre...]
    all_gather x2 -> x0, blocking collectives: 22.5 us -> none  [the longest x1 15.1 us: shards(): piece = lax.all_gather(factor_b, 'ka', axis=0, tiled=True)]
    dot_general x1 -> x0, local copies, waits for them, and re-layouts: 6.71 us -> none  [shards(): jnp.dot(tensor.reshape(rows_i * rows_j, rows_k), c_block.reshape(rows_k,...]
  transfers between devices with their start and end apart: 1 -> 0, of which waited for: 0 -> 0; matrix products, arithmetic and copies ran while one was open for 12% -> 0% of each run, Pallas kernels for 0% -> 0%
where the time goes in v1:
time: 35.4 us; the launch traced here: 35.1 us
  Pallas kernels  32 us (90%)
  local copies, waits for them, and re-layouts  2.53 us (7%)
  between operations  0.64 us (2%)
    pallas_call x1, Pallas kernels, shards(): pl.pallas_call(functools.partial(kernel, sizes, places, rows_i * na), out...  32 us
    unnamed x2, local copies, waits for them, and re-layouts  2.53 us

profile of v1, /device:TPU:0, one launch (start us, length us, event | category | flops | bytes accessed | tf_op | source)
XLA Modules:
  0.0 35.1 jit_solution(8860438917000192909)
XLA Ops:
  0.6 32.0 %factor_update.1 = (f32[4,4,96]{2,1,0:T(4,128)}, f32[4,96]{1,0:T(4,128)}) custom-call(f32[32,128,128]{2,1,0:T(8,128)} %t_ref.1, f32[32,4,96]{2,1,0:T(4,128)} %b_ref.1, f32[64,4,96]{2,1,0:T(4,128)} %c_ref.1), custom_call_target="tpu_custom_call" | custom-call | tf_op jit(solution)/shard_map/factor_update/pallas_call | solution.py:260
  32.6 1.3 %copy.7 = f32[4,4,96]{2,1,0:T(4,128)} copy(f32[4,4,96]{2,1,0:T(4,128)} %get-tuple-element.4) | data formatting | bytes 12288
  33.9 1.2 %copy.8 = f32[4,96]{1,0:T(4,128)} copy(f32[4,96]{1,0:T(4,128)} %get-tuple-element.5) | data formatting | bytes 3072

commit v2 on v1

--- a/solution.py
+++ b/solution.py
@@ -61,15 +61,15 @@
     return hi, (x - hi.astype(jnp.float32)).astype(jnp.bfloat16)
 
 
-def kernel(sizes, places, total_rows, t_ref, b_ref, c_ref, out_ref, w_ref,
-           bg, cg, gb, gc, mp, mr, ob, orx,
-           bs, br, cs, cr, gs, gbr, gcr, ms, mrs, os, ors):
+def kernel(sizes, places, total_rows, own_rows, t_hbm, b_hbm, c_hbm, res,
+           tv, bv, cv, bg, cg, bp, cp, gb, gc, mp, mr, ob, orx, inv,
+           ts, ins, bs, br, cs, cr, gs, gbr, gcr, ms, mrs, os, ors):
     na, nj, nk = sizes
     group = nj * nk
     n = na * group
-    starts, cols = b_ref.shape[1], b_ref.shape[2]
-    rows_i = t_ref.shape[0]
-    own_rows = out_ref.shape[0]
+    starts, cols = bv.shape[1], bv.shape[2]
+    rows_b = bv.shape[0]
+    rows_i, rows_j, rows_k = tv.shape
     ia, ja, ka = (lax.axis_index("ia"), lax.axis_index("ja"), lax.axis_index("ka"))
     g = ja * nk + ka
     me = ia * group + g
@@ -83,33 +83,44 @@
     def greet(target):
         pl.semaphore_signal(barrier, inc=1, device_id=target, device_id_type=MESH)
 
-    for o in range(1, nk):
-        greet((ia, ja, lax.rem(ka + o, nk)))
-    for o in range(1, nj):
-        greet((ia, lax.rem(ja + o, nj), ka))
-    for s, place in enumerate(places):
-        @pl.when(me != ids[s])
-        def _():
-            greet(place)
-
+    for s in range(starts):
         @pl.when(me == ids[s])
         def _():
             @pl.loop(1, n)
             def _(o):
                 greet(coords(lax.rem(me + o, n)))
-
-    for s in range(starts):
-        bg[ka, s] = jnp.zeros(bg.shape[2:], jnp.float32)
-        cg[ja, s] = jnp.zeros(cg.shape[2:], jnp.float32)
-        bg[ka, s, :, 0:cols] = b_ref[:, s, :]
-        cg[ja, s, :, 0:cols] = c_ref[:, s, :]
+    for o in range(1, nk):
+        greet((ia, ja, lax.rem(ka + o, nk)))
+    for o in range(1, nj):
+        greet((ia, lax.rem(ja + o, nj), ka))
+
+    load_b = pltpu.make_async_copy(b_hbm, bv, ins.at[0])
+    load_c = pltpu.make_async_copy(c_hbm, cv, ins.at[1])
+    load_t = pltpu.make_async_copy(t_hbm, tv, ts)
+    load_b.start()
+    load_c.start()
+    load_t.start()
+
+    bp[...] = jnp.zeros(bp.shape, jnp.float32)
+    cp[...] = jnp.zeros(cp.shape, jnp.float32)
+    mp[...] = jnp.zeros(mp.shape, jnp.float32)
+    load_b.wait()
+    for s in range(starts):
+        rows = bv[:, s, :]
+        bp[s, :, 0:cols] = rows
+        bg[ka, :, s * cols : (s + 1) * cols] = rows
+    load_c.wait()
+    for s in range(starts):
+        rows = cv[:, s, :]
+        cp[s, :, 0:cols] = rows
+        cg[ja, :, s * cols : (s + 1) * cols] = rows
 
     is_solver = functools.reduce(jnp.logical_or, [me == d for d in ids])
     near = (nk - 1) + (nj - 1)
 
     @pl.when(is_solver)
     def _():
-        pl.semaphore_wait(barrier, near + starts - 1 + n - 1)
+        pl.semaphore_wait(barrier, near + starts - 1)
 
     @pl.when(jnp.logical_not(is_solver))
     def _():
@@ -135,11 +146,11 @@
         for s, place in enumerate(places):
             @pl.when(ia == place[0])
             def _():
-                push(bg.at[ka, s], gb.at[g], gs.at[s], gbr, place, ids[s], act)
+                push(bp.at[s], gb.at[g], gs.at[s], gbr, place, ids[s], act)
 
             @pl.when(ia == place[0] + 1)
             def _():
-                push(cg.at[ja, s], gc.at[g], gs.at[s], gcr, place, ids[s], act)
+                push(cp.at[s], gc.at[g], gs.at[s], gcr, place, ids[s], act)
 
     gram_rows("start")
     c_copies = []
@@ -154,62 +165,70 @@
             device_id=(ia, ja, lax.rem(ka + o, nk)), device_id_type=MESH))
     for copy in c_copies + b_copies:
         copy.start()
-    for o in range(1, nj):
-        src = cg.at[lax.rem(ja - o + nj, nj)]
-        pltpu.make_async_copy(src, src, cr.at[o - 1]).wait()
-    for o in range(1, nk):
-        src = bg.at[lax.rem(ka - o + nk, nk)]
-        pltpu.make_async_copy(src, src, br.at[o - 1]).wait()
-
-    c_all = [jnp.concatenate([cg[q, s] for q in range(nj)], axis=0) for s in range(starts)]
-    c_hi, c_lo = split(jnp.concatenate(c_all, axis=1))
-    c_twice = jnp.concatenate([c_hi, c_hi], axis=0)
-    b_all = jnp.concatenate(
-        [jnp.concatenate([bg[q, s] for q in range(nk)], axis=0) for s in range(starts)], axis=1)
-    rows_j, rows_k = t_ref.shape[1], t_ref.shape[2]
-    step = SUBS
-
-    @pl.loop(0, rows_i // step)
-    def _(block):
-        at = pl.multiple_of(block * step, step)
-        t_hi, t_lo = split(t_ref[pl.ds(at, step)].reshape(step * rows_j, rows_k))
-        part = jnp.dot(jnp.concatenate([t_hi, t_lo], axis=1), c_twice,
-                       preferred_element_type=jnp.float32)
-        part = part + jnp.dot(t_hi, c_lo, preferred_element_type=jnp.float32)
-        summed = jnp.sum(part.reshape(step, rows_j, starts * LANES) * b_all[None], axis=1)
-        for s in range(starts):
-            mp[s, pl.ds(at, step), :] = summed[:, s * LANES : (s + 1) * LANES]
-
-    def mttkrp_rows(act):
-        for s, place in enumerate(places):
-            push(mp.at[s], mr.at[me], ms.at[s], mrs, place, ids[s], act)
-
-    mttkrp_rows("start")
 
     @pl.when(is_solver)
     def _():
         pltpu.make_async_copy(gb, gb, gbr).wait()
         pltpu.make_async_copy(gc, gc, gcr).wait()
         over_rows = (((0,), (0,)), ((), ()))
-        rows_b = gb[...].reshape(gb.shape[0] * gb.shape[1], LANES)
-        rows_c = gc[...].reshape(gc.shape[0] * gc.shape[1], LANES)
-        gram_b = lax.dot_general(rows_b, rows_b, over_rows, precision=HIGHEST,
+        rows_of_b = gb[...].reshape(gb.shape[0] * gb.shape[1], LANES)
+        rows_of_c = gc[...].reshape(gc.shape[0] * gc.shape[1], LANES)
+        gram_b = lax.dot_general(rows_of_b, rows_of_b, over_rows, precision=HIGHEST,
                                  preferred_element_type=jnp.float32)
-        gram_c = lax.dot_general(rows_c, rows_c, over_rows, precision=HIGHEST,
+        gram_c = lax.dot_general(rows_of_c, rows_of_c, over_rows, precision=HIGHEST,
                                  preferred_element_type=jnp.float32)
         normal = gram_b * gram_c
         tiles = [normal[i : i + SUBS, :] for i in range(0, cols, SUBS)]
         tiles = negative_inverse(tiles, cols)
-        minus = jnp.concatenate(
-            tiles + [jnp.zeros((LANES - cols, LANES), jnp.float32)], axis=0)
-
+        inv[0:cols, :] = jnp.concatenate(tiles, axis=0)
+        inv[cols:LANES, :] = jnp.zeros((LANES - cols, LANES), jnp.float32)
+
+    for o in range(1, nj):
+        src = cg.at[lax.rem(ja - o + nj, nj)]
+        pltpu.make_async_copy(src, src, cr.at[o - 1]).wait()
+    load_t.wait()
+
+    c_hi, c_lo = split(cg[...].reshape(rows_k, starts * cols))
+    c_twice = jnp.concatenate([c_hi, c_hi], axis=0)
+    acc = None
+    for o in range(nk):
+        q = lax.rem(ka - o + nk, nk)
+        if o:
+            src = bg.at[q]
+            pltpu.make_async_copy(src, src, br.at[o - 1]).wait()
+        at = pl.multiple_of(q * rows_b, rows_b)
+        b_rows = bg[q]
+        part = []
+        for i in range(0, rows_i, SUBS):
+            t_hi, t_lo = split(
+                tv[i : i + SUBS, pl.ds(at, rows_b), :].reshape(SUBS * rows_b, rows_k))
+            prod = jnp.dot(jnp.concatenate([t_hi, t_lo], axis=1), c_twice,
+                           preferred_element_type=jnp.float32)
+            prod = prod + jnp.dot(t_hi, c_lo, preferred_element_type=jnp.float32)
+            part.append(jnp.sum(
+                prod.reshape(SUBS, rows_b, starts * cols) * b_rows[None], axis=1))
+        part = jnp.concatenate(part, axis=0)
+        acc = part if acc is None else acc + part
+    for s in range(starts):
+        mp[s, :, 0:cols] = acc[:, s * cols : (s + 1) * cols]
+
+    def mttkrp_rows(act):
+        for s, place in enumerate(places):
+            push(mp.at[s], mr.at[me], ms.at[s], mrs, place, ids[s], act)
+
+    mttkrp_rows("start")
+
+    @pl.when(is_solver)
+    def _():
         pltpu.make_async_copy(mr, mr, mrs).wait()
         blocks = []
         for q in range(na):
-            blocks.append(lax.fori_loop(
-                1, group, lambda h, acc, q=q: acc + mr[q * group + h], mr[q * group]))
+            total = mr[q * group]
+            for h in range(1, group):
+                total = total + mr[q * group + h]
+            blocks.append(total)
         mttkrp = jnp.concatenate(blocks, axis=0)
-        raw = -jnp.dot(mttkrp, minus, precision=HIGHEST, preferred_element_type=jnp.float32)
+        raw = -jnp.dot(mttkrp, inv[...], precision=HIGHEST, preferred_element_type=jnp.float32)
         weight = jnp.sqrt(jnp.sum(raw * raw, axis=0, keepdims=True) / total_rows + 1e-06)
         final = raw / weight
         for d in range(n):
@@ -230,8 +249,7 @@
 
     for s in range(starts):
         pltpu.make_async_copy(orx.at[s], orx.at[s], ors.at[s]).wait()
-        out_ref[:, s, :] = orx[s, 0:own_rows, 0:cols]
-        w_ref[s : s + 1, :] = orx[s, own_rows : own_rows + 1, 0:cols]
+    res[...] = orx[...]
 
     gram_rows("wait")
     mttkrp_rows("wait")
@@ -242,6 +260,13 @@
     def _():
         rest = ob.at[pl.ds(0, n - 1)]
         pltpu.make_async_copy(rest, rest, os).wait()
+
+
+def place_kernel(res, out_ref, w_ref):
+    own_rows, starts, cols = out_ref.shape
+    for s in range(starts):
+        out_ref[:, s, :] = res[s, 0:own_rows, 0:cols]
+        w_ref[s : s + 1, :] = res[s, own_rows : own_rows + 1, 0:cols]
 
 
 def shards(sizes, tensor, factor_b, factor_c):
@@ -257,23 +282,27 @@
     dma = pltpu.SemaphoreType.DMA
     f32 = jnp.float32
     vmem = pl.BlockSpec(memory_space=pltpu.VMEM)
-    return pl.pallas_call(
-        functools.partial(kernel, sizes, places, rows_i * na),
-        out_shape=(
-            jax.ShapeDtypeStruct((own_rows, starts, cols), f32),
-            jax.ShapeDtypeStruct((starts, cols), f32),
-        ),
-        in_specs=[vmem] * 3,
-        out_specs=(vmem, vmem),
+    res = pl.pallas_call(
+        functools.partial(kernel, sizes, places, rows_i * na, own_rows),
+        out_shape=jax.ShapeDtypeStruct((starts, deep, LANES), f32),
+        in_specs=[pl.BlockSpec(memory_space=pl.ANY)] * 3,
+        out_specs=vmem,
         scratch_shapes=[
-            pltpu.VMEM((nk, starts, rows_b, LANES), f32),
-            pltpu.VMEM((nj, starts, rows_c, LANES), f32),
+            pltpu.VMEM(tensor.shape, f32),
+            pltpu.VMEM(factor_b.shape, f32),
+            pltpu.VMEM(factor_c.shape, f32),
+            pltpu.VMEM((nk, rows_b, starts * cols), f32),
+            pltpu.VMEM((nj, rows_c, starts * cols), f32),
+            pltpu.VMEM((starts, rows_b, LANES), f32),
+            pltpu.VMEM((starts, rows_c, LANES), f32),
             pltpu.VMEM((group, rows_b, LANES), f32),
             pltpu.VMEM((group, rows_c, LANES), f32),
             pltpu.VMEM((starts, rows_i, LANES), f32),
             pltpu.VMEM((n, rows_i, LANES), f32),
             pltpu.VMEM((n, deep, LANES), f32),
             pltpu.VMEM((starts, deep, LANES), f32),
+            pltpu.VMEM((LANES, LANES), f32),
+            dma, dma((2,)),
             dma((max(nk - 1, 1),)), dma((max(nk - 1, 1),)),
             dma((max(nj - 1, 1),)), dma((max(nj - 1, 1),)),
             dma((starts,)), dma, dma,
@@ -283,6 +312,16 @@
         compiler_params=pltpu.CompilerParams(collective_id=0, has_side_effects=True),
         name="factor_update",
     )(tensor, factor_b, factor_c)
+    return pl.pallas_call(
+        place_kernel,
+        out_shape=(
+            jax.ShapeDtypeStruct((own_rows, starts, cols), f32),
+            jax.ShapeDtypeStruct((starts, cols), f32),
+        ),
+        in_specs=[vmem],
+        out_specs=(vmem, vmem),
+        name="place_rows",
+    )(res)
 
 
 def solution(mesh):

time: 35.4 us -> 32.5 us (0.918)
  local copies, waits for them, and re-layouts: 2.53 us -> 0 us
    unnamed x2 -> x0, local copies, waits for them, and re-layouts: 2.53 us -> none
    pallas_call x1 -> x2, Pallas kernels: 32 us -> 31.7 us  [the longest x1 30.3 us: shards(): pl.pallas_call(functools.partial(kernel, sizes, places, rows_i * na, own_...]
where the time goes in v2:
time: 32.5 us; the launch traced here: 32.3 us
  Pallas kernels  31.7 us (98%)
  between operations  0.64 us (2%)
    pallas_call x1, Pallas kernels, shards(): pl.pallas_call(functools.partial(kernel, sizes, places, rows_i * na, own_...  30.3 us
    pallas_call x1, Pallas kernels, shards(): pl.pallas_call(place_kernel, out_shape=(jax.ShapeDtypeStruct((own_rows, s...  1.33 us

profile of v2, /device:TPU:0, one launch (start us, length us, event | category | flops | bytes accessed | tf_op | source)
XLA Modules:
  0.0 32.3 jit_solution(10977455022369065505)
XLA Ops:
  0.6 30.3 %factor_update.1.res = f32[4,8,128]{2,1,0:T(8,128)} custom-call(f32[32,128,128]{2,1,0:T(8,128)} %t_hbm.1, f32[32,4,96]{2,1,0:T(4,128)} %b_hbm.1, f32[64,4,96]{2,1,0:T(4,128)} %c_hbm.1), custom_call_target="tpu_custom_call" | custom-call | tf_op jit(solution)/shard_map/factor_update/pallas_call | solution.py:285
  31.0 1.3 %place_rows.1 = (f32[4,4,96]{2,1,0:T(4,128)}, f32[4,96]{1,0:T(4,128)}) custom-call(f32[4,8,128]{2,1,0:T(8,128)} %factor_update.1.res), custom_call_target="tpu_custom_call" | custom-call | tf_op jit(solution)/shard_map/place_rows/pallas_call | solution.py:315

commit v3 on v2

--- a/solution.py
+++ b/solution.py
@@ -10,6 +10,7 @@
 MESH = pl.DeviceIdType.MESH
 LANES = 128
 SUBS = 8
+UNROLLED = 64
 HIGHEST = lax.Precision.HIGHEST
 
 
@@ -25,35 +26,60 @@
     return places
 
 
+def spread(row, k):
+    return jnp.broadcast_to(row[:, k : k + 1], (SUBS, LANES))
+
+
+def inverse_2x2(a, b, d):
+    scale = 1.0 / (a * d - b * b)
+    return d * scale, -b * scale, a * scale
+
+
 def negative_inverse(tiles, cols):
     lane = lax.broadcasted_iota(jnp.int32, (SUBS, LANES), 1)
     sub = lax.broadcasted_iota(jnp.int32, (SUBS, LANES), 0)
-    for k in range(0, cols, 2):
+    for k in range(0, cols, 4):
         v, p = k // SUBS, k % SUBS
-        at0, at1 = lane == k, lane == k + 1
-        both = at0 | at1
-        row0 = jnp.broadcast_to(tiles[v][p : p + 1, :], (SUBS, LANES))
-        row1 = jnp.broadcast_to(tiles[v][p + 1 : p + 2, :], (SUBS, LANES))
-        col0 = [jnp.broadcast_to(t[:, k : k + 1], (SUBS, LANES)) for t in tiles]
-        col1 = [jnp.broadcast_to(t[:, k + 1 : k + 2], (SUBS, LANES)) for t in tiles]
-        a = jnp.broadcast_to(row0[:, k : k + 1], (SUBS, LANES))
-        b = jnp.broadcast_to(row0[:, k + 1 : k + 2], (SUBS, LANES))
-        d = jnp.broadcast_to(row1[:, k + 1 : k + 2], (SUBS, LANES))
-        inv_a = 1.0 / a
-        t = b * inv_a
-        inv_s = 1.0 / (d - b * t)
-        row0 = jnp.where(at0, -1.0, jnp.where(at1, 0.0, row0))
-        row1 = jnp.where(at1, -1.0, jnp.where(at0, 0.0, row1))
-        new1 = (row1 - t * row0) * inv_s
-        new0 = row0 * inv_a - t * new1
+        inside = (lane >= k) & (lane < k + 4)
+        rows = [jnp.broadcast_to(tiles[v][p + m : p + m + 1, :], (SUBS, LANES)) for m in range(4)]
+        e = {(m, q): spread(rows[m], k + q) for m in range(4) for q in range(m, 4)}
+        cols_of = [[spread(t, k + m) for m in range(4)] for t in tiles]
+        r0, r1, r2, r3 = [
+            jnp.where(inside, jnp.where(lane == k + m, -1.0, 0.0), rows[m]) for m in range(4)]
+        a00, a01, a11 = inverse_2x2(e[0, 0], e[0, 1], e[1, 1])
+        w00 = a00 * e[0, 2] + a01 * e[1, 2]
+        w01 = a00 * e[0, 3] + a01 * e[1, 3]
+        w10 = a01 * e[0, 2] + a11 * e[1, 2]
+        w11 = a01 * e[0, 3] + a11 * e[1, 3]
+        s00, s01, s11 = inverse_2x2(
+            e[2, 2] - (e[0, 2] * w00 + e[1, 2] * w10),
+            e[2, 3] - (e[0, 2] * w01 + e[1, 2] * w11),
+            e[3, 3] - (e[0, 3] * w01 + e[1, 3] * w11))
+        y2 = r2 - (w00 * r0 + w10 * r1)
+        y3 = r3 - (w01 * r0 + w11 * r1)
+        x0 = a00 * r0 + a01 * r1
+        x1 = a01 * r0 + a11 * r1
+        z2 = s00 * y2 + s01 * y3
+        z3 = s01 * y2 + s11 * y3
+        z0 = x0 - (w00 * z2 + w01 * z3)
+        z1 = x1 - (w10 * z2 + w11 * z3)
         out = []
         for i, tile in enumerate(tiles):
-            new = jnp.where(both, 0.0, tile) - col0[i] * new0 - col1[i] * new1
+            c0, c1, c2, c3 = cols_of[i]
+            new = (jnp.where(inside, 0.0, tile) - (c0 * z0 + c1 * z1)) - (c2 * z2 + c3 * z3)
             if i == v:
-                new = jnp.where(sub == p, new0, jnp.where(sub == p + 1, new1, new))
+                for m, z in enumerate((z0, z1, z2, z3)):
+                    new = jnp.where(sub == p + m, z, new)
             out.append(new)
         tiles = out
     return tiles
+
+
+def unit_scales(normal, cols):
+    at = [lax.broadcasted_iota(jnp.int32, normal.shape, a) for a in (0, 1)]
+    marked = jnp.where(at[0] == at[1], jnp.where(at[0] < cols, normal, 1.0), 0.0)
+    return (lax.rsqrt(jnp.sum(marked, axis=0, keepdims=True)),
+            lax.rsqrt(jnp.sum(marked, axis=1, keepdims=True)))
 
 
 def split(x):
@@ -178,9 +204,11 @@
         gram_c = lax.dot_general(rows_of_c, rows_of_c, over_rows, precision=HIGHEST,
                                  preferred_element_type=jnp.float32)
         normal = gram_b * gram_c
+        scale_row, scale_col = unit_scales(normal, cols)
+        normal = normal * scale_row * scale_col
         tiles = [normal[i : i + SUBS, :] for i in range(0, cols, SUBS)]
         tiles = negative_inverse(tiles, cols)
-        inv[0:cols, :] = jnp.concatenate(tiles, axis=0)
+        inv[0:cols, :] = jnp.concatenate(tiles, axis=0) * scale_row * scale_col[0:cols]
         inv[cols:LANES, :] = jnp.zeros((LANES - cols, LANES), jnp.float32)
 
     for o in range(1, nj):
@@ -240,12 +268,19 @@
             def _():
                 pltpu.make_async_copy(ob.at[me], orx.at[s], ors.at[s]).start()
 
-                @pl.loop(1, n)
-                def _(o):
-                    d = lax.rem(me + o, n)
+                def send(d):
                     pltpu.make_async_remote_copy(
                         src_ref=ob.at[d], dst_ref=orx.at[s], send_sem=os, recv_sem=ors.at[s],
                         device_id=coords(d), device_id_type=MESH).start()
+
+                if n <= UNROLLED:
+                    for d in range(n - 1, -1, -1):
+                        if d != ids[s]:
+                            send(d)
+                else:
+                    @pl.loop(1, n)
+                    def _(o):
+                        send(lax.rem(me + o, n))
 
     for s in range(starts):
         pltpu.make_async_copy(orx.at[s], orx.at[s], ors.at[s]).wait()

time: 32.5 us -> 28.4 us (0.87)
  Pallas kernels: 31.7 us -> 27.5 us
    pallas_call x1, Pallas kernels: 30.3 us -> 26.2 us  [shards(): pl.pallas_call(functools.partial(kernel, sizes, places, rows_i * na, own_...]
where the time goes in v3:
time: 28.4 us; the launch traced here: 28.2 us
  Pallas kernels  27.5 us (97%)
  between operations  0.64 us (2%)
    pallas_call x1, Pallas kernels, shards(): pl.pallas_call(functools.partial(kernel, sizes, places, rows_i * na, own_...  26.2 us
    pallas_call x1, Pallas kernels, shards(): pl.pallas_call(place_kernel, out_shape=(jax.ShapeDtypeStruct((own_rows, s...  1.33 us

profile of v3, /device:TPU:0, one launch (start us, length us, event | category | flops | bytes accessed | tf_op | source)
XLA Modules:
  0.0 28.2 jit_solution(7884144480415198551)
XLA Ops:
  0.6 26.2 %factor_update.1.res = f32[4,8,128]{2,1,0:T(8,128)} custom-call(f32[32,128,128]{2,1,0:T(8,128)} %t_hbm.1, f32[32,4,96]{2,1,0:T(4,128)} %b_hbm.1, f32[64,4,96]{2,1,0:T(4,128)} %c_hbm.1), custom_call_target="tpu_custom_call" | custom-call | tf_op jit(solution)/shard_map/factor_update/pallas_call | solution.py:320
  26.8 1.3 %place_rows.1 = (f32[4,4,96]{2,1,0:T(4,128)}, f32[4,96]{1,0:T(4,128)}) custom-call(f32[4,8,128]{2,1,0:T(8,128)} %factor_update.1.res), custom_call_target="tpu_custom_call" | custom-call | tf_op jit(solution)/shard_map/place_rows/pallas_call | solution.py:350

commit v4 on v3

--- a/solution.py
+++ b/solution.py
@@ -35,10 +35,10 @@
     return d * scale, -b * scale, a * scale
 
 
-def negative_inverse(tiles, cols):
+def negative_inverse(tiles, first, last):
     lane = lax.broadcasted_iota(jnp.int32, (SUBS, LANES), 1)
     sub = lax.broadcasted_iota(jnp.int32, (SUBS, LANES), 0)
-    for k in range(0, cols, 4):
+    for k in range(first, last, 4):
         v, p = k // SUBS, k % SUBS
         inside = (lane >= k) & (lane < k + 4)
         rows = [jnp.broadcast_to(tiles[v][p + m : p + m + 1, :], (SUBS, LANES)) for m in range(4)]
@@ -88,7 +88,7 @@
 
 
 def kernel(sizes, places, total_rows, own_rows, t_hbm, b_hbm, c_hbm, res,
-           tv, bv, cv, bg, cg, bp, cp, gb, gc, mp, mr, ob, orx, inv,
+           tv, bv, cv, bg, cg, bp, cp, gb, gc, mp, mr, ob, orx, inv, scales,
            ts, ins, bs, br, cs, cr, gs, gbr, gcr, ms, mrs, os, ors):
     na, nj, nk = sizes
     group = nj * nk
@@ -143,6 +143,7 @@
 
     is_solver = functools.reduce(jnp.logical_or, [me == d for d in ids])
     near = (nk - 1) + (nj - 1)
+    early = cols // 2 // SUBS * SUBS
 
     @pl.when(is_solver)
     def _():
@@ -207,8 +208,10 @@
         scale_row, scale_col = unit_scales(normal, cols)
         normal = normal * scale_row * scale_col
         tiles = [normal[i : i + SUBS, :] for i in range(0, cols, SUBS)]
-        tiles = negative_inverse(tiles, cols)
-        inv[0:cols, :] = jnp.concatenate(tiles, axis=0) * scale_row * scale_col[0:cols]
+        tiles = negative_inverse(tiles, 0, early)
+        inv[0:cols, :] = jnp.concatenate(tiles, axis=0)
+        scales[0] = jnp.broadcast_to(scale_row, scales.shape[1:])
+        scales[1] = jnp.broadcast_to(scale_col, scales.shape[1:])
         inv[cols:LANES, :] = jnp.zeros((LANES - cols, LANES), jnp.float32)
 
     for o in range(1, nj):
@@ -248,6 +251,9 @@
 
     @pl.when(is_solver)
     def _():
+        tiles = [inv[i : i + SUBS, :] for i in range(0, cols, SUBS)]
+        tiles = negative_inverse(tiles, early, cols)
+        inv[0:cols, :] = jnp.concatenate(tiles, axis=0) * scales[0, 0:cols] * scales[1, 0:cols]
         pltpu.make_async_copy(mr, mr, mrs).wait()
         blocks = []
         for q in range(na):
@@ -274,7 +280,7 @@
                         device_id=coords(d), device_id_type=MESH).start()
 
                 if n <= UNROLLED:
-                    for d in range(n - 1, -1, -1):
+                    for d in sorted(range(n), key=lambda d: sum(coords(d))):
                         if d != ids[s]:
                             send(d)
                 else:
@@ -337,6 +343,7 @@
             pltpu.VMEM((n, deep, LANES), f32),
             pltpu.VMEM((starts, deep, LANES), f32),
             pltpu.VMEM((LANES, LANES), f32),
+            pltpu.VMEM((2, LANES, LANES), f32),
             dma, dma((2,)),
             dma((max(nk - 1, 1),)), dma((max(nk - 1, 1),)),
             dma((max(nj - 1, 1),)), dma((max(nj - 1, 1),)),

time: 28.4 us -> 26.5 us (0.933)
  Pallas kernels: 27.5 us -> 25.7 us
    pallas_call x1, Pallas kernels: 26.2 us -> 24.3 us  [shards(): pl.pallas_call(functools.partial(kernel, sizes, places, rows_i * na, own_...]
where the time goes in v4:
time: 26.5 us; the launch traced here: 26.3 us
  Pallas kernels  25.7 us (97%)
  between operations  0.64 us (2%)
    pallas_call x1, Pallas kernels, shards(): pl.pallas_call(functools.partial(kernel, sizes, places, rows_i * na, own_...  24.3 us
    pallas_call x1, Pallas kernels, shards(): pl.pallas_call(place_kernel, out_shape=(jax.ShapeDtypeStruct((own_rows, s...  1.33 us

profile of v4, /device:TPU:0, one launch (start us, length us, event | category | flops | bytes accessed | tf_op | source)
XLA Modules:
  0.0 26.3 jit_solution(16022227591318906859)
XLA Ops:
  0.6 24.3 %factor_update.1.res = f32[4,8,128]{2,1,0:T(8,128)} custom-call(f32[32,128,128]{2,1,0:T(8,128)} %t_hbm.1, f32[32,4,96]{2,1,0:T(4,128)} %b_hbm.1, f32[64,4,96]{2,1,0:T(4,128)} %c_hbm.1), custom_call_target="tpu_custom_call" | custom-call | tf_op jit(solution)/shard_map/factor_update/pallas_call | solution.py:326
  25.0 1.3 %place_rows.1 = (f32[4,4,96]{2,1,0:T(4,128)}, f32[4,96]{1,0:T(4,128)}) custom-call(f32[4,8,128]{2,1,0:T(8,128)} %factor_update.1.res), custom_call_target="tpu_custom_call" | custom-call | tf_op jit(solution)/shard_map/place_rows/pallas_call | solution.py:357
